TPU v7x, 32 devices: a whole 2x2x4 slice. The times are simulated.
32 devices in a mesh: grp: 2 (over y), ti: 4 (over x, core), tj: 4 (over z).
Axes of the slice: x: 2, y: 2, z: 4, core: 2. Of those that a mesh axis runs over, the one named last changes fastest.
Arguments:
- corpus: bfloat16 [2, 24576, 1024], P('grp', ('ti', 'tj')), may hold values from -64 to 64
- slot_of_row: int32 [2, 24576], P('grp', ('ti', 'tj')), may hold values from -1 to 24575, as said below
Outputs:
- max_similarity: float32 [2, 12288], P('grp', ('ti', 'tj'))
Inputs may be any that keep to these rules, and one draw needn't show every extreme that they name: `slot_of_row`: every value from 0 to 24575 appears exactly once; a row with value v lies on a device whose ti index is (v % 12288) // 3072; from one device at most 192 rows have values in one aligned group of 768 consecutive values, and some device sends exactly 192 to some group.
All inputs are finite; a program needn't handle non-finite values.
Results may differ from a plain program's by a relative error of at most 0.0009.
Values may be sent and summed in bfloat16 or wider, within the bound.
A program may use at most 64 MiB of HBM per device.

v0:
```python
import jax
import jax.numpy as jnp
from jax import lax
from jax.sharding import PartitionSpec as P

BLK = 3072
epsilon = 1e-06


def per_device(corpus, slot_of_row):
    rows_in = corpus[0]
    values = slot_of_row[0]
    src_count = values.shape[0]
    features = rows_in.shape[1]
    lane_count = lax.axis_size("tj")
    sub_rows = src_count // 2
    cluster = BLK * lax.axis_size("ti")
    capacity = BLK // (lane_count * lane_count)
    owners = 2 * lane_count
    member = values >= 0
    inside = values % cluster
    grid_of = values // cluster
    sub_index = inside % BLK // sub_rows
    owner_of = jnp.where(member, grid_of * lane_count + sub_index, owners)
    onehot = (owner_of[:, None] == jnp.arange(owners, dtype=jnp.int32)[None, :]).astype(jnp.int32)
    rank_in = jnp.sum((jnp.cumsum(onehot, axis=0) - onehot) * onehot, axis=1)
    slot_pos = jnp.where(member, owner_of * capacity + rank_in, owners * capacity)
    send_rows = (
        jnp.zeros((owners * capacity, features), rows_in.dtype)
        .at[slot_pos]
        .set(rows_in, mode="drop")
    )
    send_ids = (
        jnp.full((owners * capacity,), sub_rows, jnp.int32)
        .at[slot_pos]
        .set(inside % sub_rows, mode="drop")
    )
    got_rows, got_ids = (
        lax.all_to_all(
            send_rows.reshape(owners, capacity, features),
            ("grp", "tj"),
            split_axis=0,
            concat_axis=0,
            tiled=True,
        ),
        lax.all_to_all(
            send_ids.reshape(owners, capacity),
            ("grp", "tj"),
            split_axis=0,
            concat_axis=0,
            tiled=True,
        ),
    )
    arrived = (
        jnp.zeros((sub_rows, features), rows_in.dtype)
        .at[got_ids.reshape(-1)]
        .set(got_rows.reshape(-1, features), mode="drop")
    )
    widened = arrived.astype(jnp.float32)
    row_squares = jnp.sum(widened * widened, axis=1, keepdims=True)
    inverse_norm = lax.rsqrt(row_squares + epsilon)
    unit_rows = (widened * inverse_norm).astype(jnp.bfloat16)
    tile_row = lax.axis_index("ti")
    tile_col = lax.axis_index("tj")
    block_rows = lax.all_gather(unit_rows, "tj", axis=0, tiled=True)
    row_slot = tile_row * BLK + jnp.arange(BLK, dtype=jnp.int32)
    portion = lax.all_gather(unit_rows, "ti", axis=0, tiled=True)
    length = portion.shape[0]
    position = jnp.arange(length, dtype=jnp.int32)
    col_slot = position // sub_rows * BLK + tile_col * sub_rows + position % sub_rows
    scores = lax.dot_general(
        block_rows, portion, (((1,), (1,)), ((), ())), preferred_element_type=jnp.float32
    )
    scores = jnp.where(row_slot[:, None] == col_slot[None, :], -2.0, scores)
    tile_best = jnp.maximum(jnp.full((BLK,), -2.0, jnp.float32), jnp.max(scores, axis=1))
    combined = lax.pmax(tile_best, "tj")
    result = lax.dynamic_slice_in_dim(combined, tile_col * sub_rows, sub_rows, 0)
    return result[None, :]


def solution(mesh):
    in_specs = (P("grp", ("ti", "tj"), None), P("grp", ("ti", "tj")))
    out_specs = P("grp", ("ti", "tj"))
    return jax.shard_map(
        per_device, mesh=mesh, in_specs=in_specs, out_specs=out_specs, check_vma=False
    )
```

profile of v0, /device:TPU:0, one launch (start us, length us, event | category | flops | bytes accessed | tf_op | source)
XLA Modules:
  0.0 336.0 jit_solution(1104900848834688039)
XLA Ops:
  6.5 0.0 copy-start
  6.5 0.9 fusion.39
  7.4 0.8 compare_reduce_fusion.1
  8.3 2.3 reduce-window.6
  10.6 0.3 slice_reduce_fusion
  10.9 0.2 reduce-window.9
  11.1 0.1 add_bitcast_fusion
  11.2 0.8 fusion.32
  12.0 6.2 %scatter_custom_fusion = s32[1536]{0:T(1024)S(1)} fusion(s32[1536]{0:T(1024)S(1)} %fusion.32, s32[1536]{0:T(1024)S(1)} %get-tuple-element.9, s32[]{:T(128)} %constant.74.clone.1), kind=kCustom, calls=%fused_computation.82 | custom fusion | bytes 6148 | tf_op jit(solution)/shard_map/scatter | solution.py:36
  18.2 0.7 all_to_all.9
  18.9 7.3 %all-to-all-start = ((s32[8,1,192]{2,1,0:T(1,128)}), s32[8,1,192]{2,1,0:T(1,128)S(1)}, u32[]{:S(2)}, u32[]{:S(2)}) async-start(s32[8,1,192]{2,1,0:T(1,128)} %all_to_all.9), calls=%async_computation | async-start | bytes 16384 | tf_op jit(solution)/shard_map/all_to_all | solution.py:46
  26.2 0.0 copy-done
  26.2 9.7 %scatter_custom_fusion.1 = bf16[1536,1024]{1,0:T(8,128)(2,1)} fusion(s32[1536]{0:T(1024)S(1)} %fusion.32, bf16[1,1536,1024]{2,1,0:T(8,128)(2,1)S(1)} %copy-done, bf16[]{:T(256)} %constant.78.clone.1), kind=kCustom, calls=%fused_computation.8 | custom fusion | bytes 6291458 | tf_op jit(solution)/shard_map/scatter | solution.py:31
  35.9 0.0 all-to-all-done
  35.9 6.0 %all-to-all-start.1 = ((bf16[8,192,1024]{2,1,0:T(8,128)(2,1)}), bf16[8,192,1024]{2,1,0:T(8,128)(2,1)}, u32[]{:S(2)}, u32[]{:S(2)}) async-start(bf16[8,192,1024]{2,1,0:T(8,128)(2,1)} %bitcast.80), calls=%async_computation.1 | async-start | bytes 6291456 | tf_op jit(solution)/shard_map/all_to_all | solution.py:39
  41.9 0.0 all-gather.3.cloned.1.call-start
  42.0 0.1 reshape.266
  42.1 70.9 %all-to-all-done.1 = bf16[8,192,1024]{2,1,0:T(8,128)(2,1)} async-done(((bf16[8,192,1024]{2,1,0:T(8,128)(2,1)}), bf16[8,192,1024]{2,1,0:T(8,128)(2,1)}, u32[]{:S(2)}, u32[]{:S(2)}) %all-to-all-start.1) | async-done | bytes 3145760 | tf_op jit(solution)/shard_map/all_to_all | solution.py:39
  113.0 9.5 %scatter_custom_fusion.2 = bf16[768,1024]{1,0:T(8,128)(2,1)} fusion(s32[1536]{0:T(1024)S(1)} %fusion.33, bf16[1536,1024]{1,0:T(8,128)(2,1)} %bitcast.7, bf16[]{:T(256)} %constant.78.clone.1), kind=kCustom, calls=%fused_computation.11 | custom fusion | bytes 1573376 | tf_op jit(solution)/shard_map/scatter | solution.py:57
  122.5 1.8 fusion
  124.2 2.9 fusion.1
  127.2 0.0 all-gather.3.cloned.1.call-update
  127.2 0.2 all-gather.5.cloned.1.call-start
  127.4 0.5 all-gather.5.cloned.1.call-update
  128.0 112.0 %all-gather.3.cloned.1.call-done = bf16[3072,1024]{1,0:T(8,128)(2,1)} async-done(((bf16[768,1024]{1,0:T(8,128)(2,1)}), bf16[3072,1024]{1,0:T(8,128)(2,1)}) %all-gather.3.cloned.1.call-update) | async-done | bytes 6291472 | tf_op jit(solution)/shard_map/all_gather | solution.py:65
  240.0 46.1 %all-gather.5.cloned.1.call-done = bf16[3072,1024]{1,0:T(8,128)(2,1)} async-done(((bf16[768,1024]{1,0:T(8,128)(2,1)}), bf16[3072,1024]{1,0:T(8,128)(2,1)}) %all-gather.5.cloned.1.call-update) | async-done | bytes 6291472 | tf_op jit(solution)/shard_map/all_gather | solution.py:67
  286.2 23.7 %select_reduce_fusion = f32[3072]{0:T(1024)S(1)} fusion(bf16[3072,1024]{1,0:T(8,128)(2,1)} %all-gather.3.cloned.1.call-done, bf16[3072,1024]{1,0:T(8,128)(2,1)} %all-gather.5.cloned.1.call-done, s32[3072]{0:T(1024)S(1)} %iota_add_fusion, s32[3072]{0:T(1024)S(1)} %fusion.20), kind=kOutput, calls=%fused_computation.3 | convolution fusion | flops 19355660288 | bytes 12619776 | tf_op jit(solution)/shard_map/dot_general | solution.py:71
  309.8 18.7 %pmax.7 = f32[3072]{0:T(1024)S(1)} all-reduce(f32[3072]{0:T(1024)S(1)} %broadcast_maximum_fusion), channel_id=1, replica_groups=mesh['grp'=2,'ti'=4,'tj'=4] {'tj'}, use_global_device_ids=true, to_apply=%region_8.9 | all-reduce | flops 3072 | bytes 24576 | tf_op jit(solution)/shard_map/pmax | solution.py:76
  328.5 0.1 dynamic_slice.3
  328.6 0.6 broadcast_in_dim.43
  (10 shorter events, 0.2 us)
Async XLA Ops:
  6.5 19.7 %copy-start = (bf16[1,1536,1024]{2,1,0:T(8,128)(2,1)S(1)}, bf16[1,1536,1024]{2,1,0:T(8,128)(2,1)}, u32[]{:S(2)}) copy-start(bf16[1,1536,1024]{2,1,0:T(8,128)(2,1)} %param.2) | copy-start | bytes 9437188
  18.9 17.0 %all-to-all-start = ((s32[8,1,192]{2,1,0:T(1,128)}), s32[8,1,192]{2,1,0:T(1,128)S(1)}, u32[]{:S(2)}, u32[]{:S(2)}) async-start(s32[8,1,192]{2,1,0:T(1,128)} %all_to_all.9), calls=%async_computation | async-start | bytes 16384 | tf_op jit(solution)/shard_map/all_to_all | solution.py:46
  35.9 77.1 %all-to-all-start.1 = ((bf16[8,192,1024]{2,1,0:T(8,128)(2,1)}), bf16[8,192,1024]{2,1,0:T(8,128)(2,1)}, u32[]{:S(2)}, u32[]{:S(2)}) async-start(bf16[8,192,1024]{2,1,0:T(8,128)(2,1)} %bitcast.80), calls=%async_computation.1 | async-start | bytes 6291456 | tf_op jit(solution)/shard_map/all_to_all | solution.py:39
  41.9 198.1 %all-gather.3.cloned.1.call-start = ((), (), s32[]{:S(2)}) async-start(), calls=%async_computation.2 | async-start | bytes 7864320 | tf_op jit(solution)/shard_map/all_gather | solution.py:65
  127.2 159.0 %all-gather.5.cloned.1.call-start = ((), (), s32[]{:S(2)}) async-start(), calls=%async_computation.3 | async-start | bytes 7864320 | tf_op jit(solution)/shard_map/all_gather | solution.py:67
Sparse Core Ops, SparseCore 0:
  127.3 112.6 all-gather.2
  241.6 44.5 all-gather.4
where the time goes:
time: 336 us
  waiting for transfers between devices  230 us (68%)
  local copies, waits for them, and re-layouts  27 us (8%)
  matrix products  23.7 us (7%)
  blocking collectives  18.7 us (6%)
  starting transfers between devices  13.6 us (4%)
  between operations  13.5 us (4%)
  other arithmetic  9.96 us (3%)
    all_gather x1, waiting for transfers between devices, per_device(): block_rows = lax.all_gather(unit_rows, 'tj', axis=0, tiled=True)  112 us
    all_to_all x1, waiting for transfers between devices, per_device(): lax.all_to_all(send_rows.reshape(owners, capacity, features), ('grp', 'tj...  70.9 us
    all_gather x1, waiting for transfers between devices, per_device(): portion = lax.all_gather(unit_rows, 'ti', axis=0, tiled=True)  46.1 us
    dot_general x1, matrix products, per_device(): lax.dot_general(block_rows, portion, (((1,), (1,)), ((), ())), preferred_...  23.7 us
    pmax x1, blocking collectives, per_device(): combined = lax.pmax(tile_best, 'tj')  18.7 us
    scatter x1, local copies, waits for them, and re-layouts, per_device(): send_rows = jnp.zeros((owners * capacity, features), rows_in.dtype).at[sl...  9.66 us
    scatter x1, local copies, waits for them, and re-layouts, per_device(): arrived = jnp.zeros((sub_rows, features), rows_in.dtype).at[got_ids.resha...  9.47 us
    all_to_all x1, starting transfers between devices, per_device(): lax.all_to_all(send_ids.reshape(owners, capacity), ('grp', 'tj'), split_a...  7.31 us
  transfers between devices with their start and end apart: 4, of which 3 were waited for; matrix products, arithmetic and copies ran while one was open for 3% of the time, Pallas kernels for 0%

commit v1 on v0

--- a/solution.py
+++ b/solution.py
@@ -64,7 +64,13 @@
     tile_col = lax.axis_index("tj")
     block_rows = lax.all_gather(unit_rows, "tj", axis=0, tiled=True)
     row_slot = tile_row * BLK + jnp.arange(BLK, dtype=jnp.int32)
-    portion = lax.all_gather(unit_rows, "ti", axis=0, tiled=True)
+    devices = lax.axis_size("ti")
+    block, blocks = (unit_rows, [unit_rows])
+    for _ in range(devices - 1):
+        block = lax.ppermute(block, "ti", [(i, (i + 1) % devices) for i in range(devices)])
+        blocks.insert(0, block)
+    flat = jnp.concatenate(blocks, axis=0)
+    portion = jnp.roll(flat, (lax.axis_index("ti") + 1) * unit_rows.shape[0], axis=0)
     length = portion.shape[0]
     position = jnp.arange(length, dtype=jnp.int32)
     col_slot = position // sub_rows * BLK + tile_col * sub_rows + position % sub_rows

time: 336 us -> 287 us (0.85)
  waiting for transfers between devices: 230 us -> 166 us
  local copies, waits for them, and re-layouts: 27 us -> 41.7 us
    all_gather x1, waiting for transfers between devices: 112 us -> 34.9 us  [per_device(): block_rows = lax.all_gather(unit_rows, 'tj', axis=0, tiled=True)]
    ppermute x0 -> x3, waiting for transfers between devices: none -> 60.1 us  [per_device(): lax.ppermute(block, 'ti', [(i, (i + 1) % devices) for i in range(devices)])]
    all_gather x1 -> x0, waiting for transfers between devices: 46.1 us -> none  [per_device(): portion = lax.all_gather(unit_rows, 'ti', axis=0, tiled=True)]
    unnamed x2 -> x14, local copies, waits for them, and re-layouts: 0.01 us -> 14.7 us
  transfers between devices with their start and end apart: 4 -> 6, of which waited for: 3 -> 5; matrix products, arithmetic and copies ran while one was open for 3% -> 9% of each run, Pallas kernels for 0% -> 0%
where the time goes in v1:
time: 287 us
  waiting for transfers between devices  166 us (58%)
  local copies, waits for them, and re-layouts  41.7 us (15%)
  matrix products  23.8 us (8%)
  blocking collectives  15.7 us (5%)
  between operations  13.5 us (5%)
  starting transfers between devices  13.4 us (5%)
  other arithmetic  12.9 us (4%)
    all_to_all x1, waiting for transfers between devices, per_device(): lax.all_to_all(send_rows.reshape(owners, capacity, features), ('grp', 'tj...  70.9 us
    ppermute x3, waiting for transfers between devices, per_device(): lax.ppermute(block, 'ti', [(i, (i + 1) % devices) for i in range(devices)])  60.1 us
    all_gather x1, waiting for transfers between devices, per_device(): block_rows = lax.all_gather(unit_rows, 'tj', axis=0, tiled=True)  34.9 us
    dot_general x1, matrix products, per_device(): lax.dot_general(block_rows, portion, (((1,), (1,)), ((), ())), preferred_...  23.8 us
    pmax x1, blocking collectives, per_device(): combined = lax.pmax(tile_best, 'tj')  15.7 us
    unnamed x14, local copies, waits for them, and re-layouts  14.7 us
    scatter x1, local copies, waits for them, and re-layouts, per_device(): send_rows = jnp.zeros((owners * capacity, features), rows_in.dtype).at[sl...  9.66 us
    scatter x1, local copies, waits for them, and re-layouts, per_device(): arrived = jnp.zeros((sub_rows, features), rows_in.dtype).at[got_ids.resha...  9.48 us
  transfers between devices with their start and end apart: 6, of which 5 were waited for; matrix products, arithmetic and copies ran while one was open for 9% of the time, Pallas kernels for 0%

profile of v1, /device:TPU:0, one launch (start us, length us, event | category | flops | bytes accessed | tf_op | source)
XLA Modules:
  0.0 287.0 jit_solution(15109673049695555482)
XLA Ops:
  6.5 0.0 copy-start
  6.5 0.9 fusion.41
  7.4 0.8 compare_reduce_fusion.1
  8.3 2.3 reduce-window.6
  10.6 0.3 slice_reduce_fusion
  10.9 0.2 reduce-window.9
  11.1 0.1 add_bitcast_fusion
  11.2 0.8 fusion.33
  12.0 6.2 %scatter_custom_fusion = s32[1536]{0:T(1024)S(1)} fusion(s32[1536]{0:T(1024)S(1)} %fusion.33, s32[1536]{0:T(1024)S(1)} %get-tuple-element.9, s32[]{:T(128)} %constant.88.clone.1), kind=kCustom, calls=%fused_computation.91 | custom fusion | bytes 6148 | tf_op jit(solution)/shard_map/scatter | solution.py:36
  18.2 0.7 all_to_all.9
  18.9 7.3 %all-to-all-start = ((s32[8,1,192]{2,1,0:T(1,128)}), s32[8,1,192]{2,1,0:T(1,128)S(1)}, u32[]{:S(2)}, u32[]{:S(2)}) async-start(s32[8,1,192]{2,1,0:T(1,128)} %all_to_all.9), calls=%async_computation | async-start | bytes 16384 | tf_op jit(solution)/shard_map/all_to_all | solution.py:46
  26.2 0.0 copy-done
  26.2 9.7 %scatter_custom_fusion.1 = bf16[1536,1024]{1,0:T(8,128)(2,1)} fusion(s32[1536]{0:T(1024)S(1)} %fusion.33, bf16[1,1536,1024]{2,1,0:T(8,128)(2,1)S(1)} %copy-done, bf16[]{:T(256)} %constant.92.clone.1), kind=kCustom, calls=%fused_computation.9 | custom fusion | bytes 6291458 | tf_op jit(solution)/shard_map/scatter | solution.py:31
  35.9 0.0 all-to-all-done
  35.9 6.0 %all-to-all-start.1 = ((bf16[8,192,1024]{2,1,0:T(8,128)(2,1)}), bf16[8,192,1024]{2,1,0:T(8,128)(2,1)}, u32[]{:S(2)}, u32[]{:S(2)}) async-start(bf16[8,192,1024]{2,1,0:T(8,128)(2,1)} %bitcast.79), calls=%async_computation.1 | async-start | bytes 6291456 | tf_op jit(solution)/shard_map/all_to_all | solution.py:39
  41.9 0.0 all-gather.2.cloned.1.call-start
  42.0 0.1 reshape.266
  42.1 70.9 %all-to-all-done.1 = bf16[8,192,1024]{2,1,0:T(8,128)(2,1)} async-done(((bf16[8,192,1024]{2,1,0:T(8,128)(2,1)}), bf16[8,192,1024]{2,1,0:T(8,128)(2,1)}, u32[]{:S(2)}, u32[]{:S(2)}) %all-to-all-start.1) | async-done | bytes 3145760 | tf_op jit(solution)/shard_map/all_to_all | solution.py:39
  113.0 9.5 %scatter_custom_fusion.2 = bf16[768,1024]{1,0:T(8,128)(2,1)} fusion(s32[1536]{0:T(1024)S(1)} %fusion.34, bf16[1536,1024]{1,0:T(8,128)(2,1)} %bitcast.7, bf16[]{:T(256)} %constant.92.clone.1), kind=kCustom, calls=%fused_computation.12 | custom fusion | bytes 1573376 | tf_op jit(solution)/shard_map/scatter | solution.py:57
  122.5 1.8 fusion.1
  124.3 2.9 %fusion.2 = bf16[768,1024]{1,0:T(8,128)(2,1)} fusion(bf16[768,1024]{1,0:T(8,128)(2,1)} %scatter_custom_fusion.2, f32[768]{0:T(1024)S(1)} %add_rsqrt_fusion), kind=kLoop, calls=%fused_computation.8 | loop fusion | flops 2359296 | bytes 3148800 | tf_op jit(solution)/shard_map/convert_element_type | solution.py:62
  127.1 0.0 all-gather.2.cloned.1.call-update
  127.2 0.1 collective-permute-start
  127.2 20.0 %collective-permute-done = bf16[768,1024]{1,0:T(8,128)(2,1)S(1)} collective-permute-done((bf16[768,1024]{1,0:T(8,128)(2,1)}, bf16[768,1024]{1,0:T(8,128)(2,1)S(1)}, u32[]{:S(2)}, u32[]{:S(2)}) %collective-permute-start) | collective-permute-done | bytes 1572896 | tf_op jit(solution)/shard_map/ppermute | solution.py:70
  147.3 0.0 copy-start.2
  147.3 1.2 copy-done.2
  148.5 0.0 collective-permute-start.1
  148.5 19.9 %collective-permute-done.1 = bf16[768,1024]{1,0:T(8,128)(2,1)} collective-permute-done((bf16[768,1024]{1,0:T(8,128)(2,1)S(1)}, bf16[768,1024]{1,0:T(8,128)(2,1)}, u32[]{:S(2)}, u32[]{:S(2)}) %collective-permute-start.1) | collective-permute-done | bytes 1572896 | tf_op jit(solution)/shard_map/ppermute | solution.py:70
  168.5 0.0 collective-permute-start.2
  168.5 0.0 copy-start.3
  168.5 20.1 %collective-permute-done.2 = bf16[768,1024]{1,0:T(8,128)(2,1)} collective-permute-done((bf16[768,1024]{1,0:T(8,128)(2,1)}, bf16[768,1024]{1,0:T(8,128)(2,1)}, u32[]{:S(2)}, u32[]{:S(2)}) %collective-permute-start.2) | collective-permute-done | bytes 1572896 | tf_op jit(solution)/shard_map/ppermute | solution.py:70
  188.6 2.7 constant_dynamic-update-slice_fusion.7
  191.3 0.0 copy-start.1
  191.3 2.8 constant_dynamic-update-slice_fusion.6
  194.1 0.0 copy-done.3
  194.1 1.3 constant_dynamic-update-slice_fusion.5
  195.4 0.0 copy-done.1
  195.4 1.5 constant_dynamic-update-slice_fusion.4
  196.9 2.7 constant_dynamic-update-slice_fusion.3
  199.5 2.8 constant_dynamic-update-slice_fusion.2
  202.3 1.3 constant_dynamic-update-slice_fusion.1
  203.6 1.5 constant_dynamic-update-slice_fusion
  205.0 34.9 %all-gather.2.cloned.1.call-done = bf16[3072,1024]{1,0:T(8,128)(2,1)} async-done(((bf16[768,1024]{1,0:T(8,128)(2,1)}), bf16[3072,1024]{1,0:T(8,128)(2,1)}) %all-gather.2.cloned.1.call-update) | async-done | bytes 6291472 | tf_op jit(solution)/shard_map/all_gather | solution.py:65
  240.0 23.8 %select_reduce_fusion = f32[3072]{0:T(1024)S(1)} fusion(bf16[3072,1024]{1,0:T(8,128)(2,1)} %all-gather.2.cloned.1.call-done, s32[3072]{0:T(1024)S(1)} %iota_add_fusion, s32[3072]{0:T(1024)S(1)} %fusion.21, bf16[6144,1024]{1,0:T(8,128)(2,1)} %constant_dynamic-update-slice_fusion, s32[]{:T(128)S(6)} %select_n.193), kind=kOutput, calls=%fused_computation.3 | convolution fusion | flops 19355660288 | bytes 12619780 | tf_op jit(solution)/shard_map/dot_general | solution.py:77
  263.8 15.7 %pmax.7 = f32[3072]{0:T(1024)S(1)} all-reduce(f32[3072]{0:T(1024)S(1)} %broadcast_maximum_fusion), channel_id=1, replica_groups=mesh['grp'=2,'ti'=4,'tj'=4] {'tj'}, use_global_device_ids=true, to_apply=%region_8.9 | all-reduce | flops 3072 | bytes 24576 | tf_op jit(solution)/shard_map/pmax | solution.py:82
  279.5 0.1 dynamic_slice.8
  279.5 0.6 broadcast_in_dim.43
  (10 shorter events, 0.2 us)
Async XLA Ops:
  6.5 19.7 %copy-start = (bf16[1,1536,1024]{2,1,0:T(8,128)(2,1)S(1)}, bf16[1,1536,1024]{2,1,0:T(8,128)(2,1)}, u32[]{:S(2)}) copy-start(bf16[1,1536,1024]{2,1,0:T(8,128)(2,1)} %param.2) | copy-start | bytes 9437188
  18.9 17.0 %all-to-all-start = ((s32[8,1,192]{2,1,0:T(1,128)}), s32[8,1,192]{2,1,0:T(1,128)S(1)}, u32[]{:S(2)}, u32[]{:S(2)}) async-start(s32[8,1,192]{2,1,0:T(1,128)} %all_to_all.9), calls=%async_computation | async-start | bytes 16384 | tf_op jit(solution)/shard_map/all_to_all | solution.py:46
  35.9 77.1 %all-to-all-start.1 = ((bf16[8,192,1024]{2,1,0:T(8,128)(2,1)}), bf16[8,192,1024]{2,1,0:T(8,128)(2,1)}, u32[]{:S(2)}, u32[]{:S(2)}) async-start(bf16[8,192,1024]{2,1,0:T(8,128)(2,1)} %bitcast.79), calls=%async_computation.1 | async-start | bytes 6291456 | tf_op jit(solution)/shard_map/all_to_all | solution.py:39
  41.9 198.1 %all-gather.2.cloned.1.call-start = ((), (), s32[]{:S(2)}) async-start(), calls=%async_computation.2 | async-start | bytes 7864320 | tf_op jit(solution)/shard_map/all_gather | solution.py:65
  127.2 20.1 %collective-permute-start = (bf16[768,1024]{1,0:T(8,128)(2,1)}, bf16[768,1024]{1,0:T(8,128)(2,1)S(1)}, u32[]{:S(2)}, u32[]{:S(2)}) collective-permute-start(bf16[768,1024]{1,0:T(8,128)(2,1)} %fusion.2), channel_id=1, source_target_pairs={{0,4},{4,8},{8,12},{12,0},{1,5},{5,9},{9,13},{13,1},{2,6},{6,10},{... | collective-permute-start | bytes 4718600 | tf_op jit(solution)/shard_map/ppermute | solution.py:70
  147.3 1.2 copy-start.2
  148.5 19.9 %collective-permute-start.1 = (bf16[768,1024]{1,0:T(8,128)(2,1)S(1)}, bf16[768,1024]{1,0:T(8,128)(2,1)}, u32[]{:S(2)}, u32[]{:S(2)}) collective-permute-start(bf16[768,1024]{1,0:T(8,128)(2,1)S(1)} %collective-permute-done), channel_id=1, source_target_pairs={{0,4},{4,8},{8,12},{12,0},{1,5},{5,9},{9,13},{13,1},{2,6},{6,10},{... | collective-permute-start | bytes 4718600 | tf_op jit(solution)/shard_map/ppermute | solution.py:70
  168.5 20.2 %collective-permute-start.2 = (bf16[768,1024]{1,0:T(8,128)(2,1)}, bf16[768,1024]{1,0:T(8,128)(2,1)}, u32[]{:S(2)}, u32[]{:S(2)}) collective-permute-start(bf16[768,1024]{1,0:T(8,128)(2,1)} %collective-permute-done.1), channel_id=1, source_target_pairs={{0,4},{4,8},{8,12},{12,0},{1,5},{5,9},{9,13},{13,1},{2,6},{6,10},{... | collective-permute-start | bytes 4718600 | tf_op jit(solution)/shard_map/ppermute | solution.py:70
  168.5 25.6 %copy-start.3 = (bf16[768,1024]{1,0:T(8,128)(2,1)S(1)}, bf16[768,1024]{1,0:T(8,128)(2,1)}, u32[]{:S(2)}) copy-start(bf16[768,1024]{1,0:T(8,128)(2,1)} %copy-done.2) | copy-start | bytes 4718596
  191.3 4.1 %copy-start.1 = (bf16[768,1024]{1,0:T(8,128)(2,1)S(1)}, bf16[768,1024]{1,0:T(8,128)(2,1)}, u32[]{:S(2)}) copy-start(bf16[768,1024]{1,0:T(8,128)(2,1)} %scatter_custom_fusion.2) | copy-start | bytes 4718596
Sparse Core Ops, SparseCore 0:
  127.3 112.6 all-gather.1
